TPU v7x, 32 devices: a whole 2x2x4 slice. The times are simulated.
32 devices in a mesh: gx: 8 (over z, core), gy: 4 (over y, x).
Axes of the slice: x: 2, y: 2, z: 4, core: 2. Of those that a mesh axis runs over, the one named last changes fastest.
Arguments:
- tokens: bfloat16 [64, 32, 8, 768], P('gx', 'gy'), may hold values from -64 to 64
- target: bfloat16 [64, 32, 8, 768], P('gx', 'gy'), may hold values from -4 to 4
- norm_gain: float32 [768], replicated, may hold values from 0.1 to 1.9
- qkv_weight: bfloat16 [768, 1152], P('gy'), may hold values from -4 to 4
- proj_weight: bfloat16 [384, 768], P('gy'), may hold values from -1.5 to 1.5
Outputs:
- block_out: bfloat16 [64, 32, 8, 768], P('gx', 'gy')
- qkv_grad: float32 [768, 1152], P('gy')
All inputs are finite; a program needn't handle non-finite values.
Results may differ from a plain program's by a relative error of at most 0.0094.
Values may be sent and summed in bfloat16 or wider, within the bound.
A program may use at most 64 MiB of HBM per device.

v0:
```python
import math
import jax
import jax.numpy as jnp
from jax import lax
from jax.sharding import PartitionSpec as P

HEADS = 12
HD = 32
WIN = 8
norm_eps = 1e-05


def shifted(x, axis, by):
    devices = lax.axis_size(axis)
    return lax.ppermute(x, axis, [(i, (i + by) % devices) for i in range(devices)])


def displace(volume, half_width):
    volume = jnp.roll(volume, -half_width, axis=2)
    upper_rows = shifted(volume[:half_width], "gx", -1)
    volume = jnp.concatenate([volume[half_width:], upper_rows], 0)
    upper_cols = shifted(volume[:, :half_width], "gy", -1)
    return jnp.concatenate([volume[:, half_width:], upper_cols], 1)


def restore(volume, half_width):
    lower_rows = shifted(volume[-half_width:], "gx", 1)
    volume = jnp.concatenate([lower_rows, volume[:-half_width]], 0)
    lower_cols = shifted(volume[:, -half_width:], "gy", 1)
    volume = jnp.concatenate([lower_cols, volume[:, :-half_width]], 1)
    return jnp.roll(volume, half_width, axis=2)


def into_windows(volume, window):
    ext_x, ext_y, ext_z, channels = volume.shape
    blocks = volume.reshape(ext_x, ext_y, ext_z // window, window, channels)
    return blocks.transpose(2, 0, 1, 3, 4).reshape(
        ext_z // window, ext_x * ext_y * window, channels
    )


def from_windows(windows, ext_x, ext_y, window):
    window_count = windows.shape[0]
    channels = windows.shape[2]
    blocks = windows.reshape(window_count, ext_x, ext_y, window, channels).transpose(1, 2, 0, 3, 4)
    return blocks.reshape(ext_x, ext_y, window_count * window, channels)


def head_probs(queries, keys_in, score_scale):
    scores = (
        jnp.einsum("wqd,wkd->wqk", queries, keys_in, preferred_element_type=jnp.float32)
        * score_scale
    )
    row_max = jnp.max(scores, -1, keepdims=True)
    exponent = jnp.exp(scores - row_max)
    return exponent / jnp.sum(exponent, -1, keepdims=True)


def shards(tokens, target, norm_gain, qkv_weight, proj_weight):
    window = WIN
    half_width = WIN // 2
    head_count = HEADS
    head_dim = HD
    inner_dim = HEADS * HD
    score_scale = HD ** (-0.5)
    ext_x, ext_y, ext_z, channels = tokens.shape
    total_tokens = ext_x * ext_y * ext_z * lax.axis_size("gx") * lax.axis_size("gy")
    loss_scale = 2.0 / math.sqrt(total_tokens)
    widened = tokens.astype(jnp.float32)
    token_mean = jnp.mean(widened, -1, keepdims=True)
    centred = widened - token_mean
    variance = jnp.mean(centred * centred, -1, keepdims=True)
    normed = (centred * lax.rsqrt(variance + norm_eps) * norm_gain).astype(jnp.bfloat16)
    windows_in = into_windows(displace(normed, half_width), window)
    window_count = windows_in.shape[0]
    window_tokens = windows_in.shape[1]
    flat_in = windows_in.reshape(-1, channels)
    qkv_whole = lax.all_gather(qkv_weight, "gy", axis=0, tiled=True)
    qkv_act = jnp.dot(flat_in, qkv_whole, preferred_element_type=jnp.float32).astype(jnp.bfloat16)
    qkv_act = qkv_act.reshape(window_count, window_tokens, 3 * inner_dim)

    def forward_head(head_idx, attn_buffer):
        queries = lax.dynamic_slice_in_dim(qkv_act, head_idx * head_dim, head_dim, 2)
        keys_in = lax.dynamic_slice_in_dim(qkv_act, inner_dim + head_idx * head_dim, head_dim, 2)
        values = lax.dynamic_slice_in_dim(qkv_act, 2 * inner_dim + head_idx * head_dim, head_dim, 2)
        attn_prob = head_probs(queries, keys_in, score_scale).astype(jnp.bfloat16)
        mixed = jnp.einsum(
            "wqk,wkd->wqd", attn_prob, values, preferred_element_type=jnp.float32
        ).astype(jnp.bfloat16)
        return lax.dynamic_update_slice_in_dim(attn_buffer, mixed, head_idx * head_dim, 2)

    attn_out = lax.fori_loop(
        0,
        head_count,
        forward_head,
        jnp.zeros((window_count, window_tokens, inner_dim), jnp.bfloat16),
    )
    proj_whole = lax.all_gather(proj_weight, "gy", axis=0, tiled=True)
    contract_cols = (((1,), (1,)), ((), ()))
    block_shift = jnp.dot(
        attn_out.reshape(-1, inner_dim), proj_whole, preferred_element_type=jnp.float32
    ).astype(jnp.bfloat16)
    block_shift = block_shift.reshape(window_count, window_tokens, channels)
    block_out = restore(from_windows(block_shift, ext_x, ext_y, window), half_width)
    grad_out = ((block_out.astype(jnp.float32) - target.astype(jnp.float32)) * loss_scale).astype(
        jnp.bfloat16
    )
    grad_shift = into_windows(displace(grad_out, half_width), window)
    grad_windows = lax.dot_general(
        grad_shift.reshape(-1, channels),
        proj_whole,
        contract_cols,
        preferred_element_type=jnp.float32,
    ).astype(jnp.bfloat16)
    grad_windows = grad_windows.reshape(window_count, window_tokens, inner_dim)

    def backward_head(head_idx, grad_buffer):
        queries = lax.dynamic_slice_in_dim(qkv_act, head_idx * head_dim, head_dim, 2)
        keys_in = lax.dynamic_slice_in_dim(qkv_act, inner_dim + head_idx * head_dim, head_dim, 2)
        values = lax.dynamic_slice_in_dim(qkv_act, 2 * inner_dim + head_idx * head_dim, head_dim, 2)
        attn_prob = head_probs(queries, keys_in, score_scale)
        prob_half = attn_prob.astype(jnp.bfloat16)
        grad_mixed = lax.dynamic_slice_in_dim(grad_windows, head_idx * head_dim, head_dim, 2)
        grad_probs = jnp.einsum(
            "wqd,wkd->wqk", grad_mixed, values, preferred_element_type=jnp.float32
        )
        grad_values = jnp.einsum(
            "wqk,wqd->wkd", prob_half, grad_mixed, preferred_element_type=jnp.float32
        ).astype(jnp.bfloat16)
        row_dot = jnp.sum(grad_probs * attn_prob, -1, keepdims=True)
        grad_scores = (attn_prob * (grad_probs - row_dot)).astype(jnp.bfloat16)
        grad_queries = (
            jnp.einsum("wqk,wkd->wqd", grad_scores, keys_in, preferred_element_type=jnp.float32)
            * score_scale
        ).astype(jnp.bfloat16)
        grad_keys = (
            jnp.einsum("wqk,wqd->wkd", grad_scores, queries, preferred_element_type=jnp.float32)
            * score_scale
        ).astype(jnp.bfloat16)
        grad_buffer = lax.dynamic_update_slice_in_dim(
            grad_buffer, grad_queries, head_idx * head_dim, 2
        )
        grad_buffer = lax.dynamic_update_slice_in_dim(
            grad_buffer, grad_keys, inner_dim + head_idx * head_dim, 2
        )
        return lax.dynamic_update_slice_in_dim(
            grad_buffer, grad_values, 2 * inner_dim + head_idx * head_dim, 2
        )

    grad_qkv = lax.fori_loop(
        0,
        head_count,
        backward_head,
        jnp.zeros((window_count, window_tokens, 3 * inner_dim), jnp.bfloat16),
    )
    grad_flat = grad_qkv.reshape(-1, 3 * inner_dim)
    contract_rows = (((0,), (0,)), ((), ()))
    shard_rows = qkv_weight.shape[0]
    local_grad = lax.dot_general(
        flat_in, grad_flat, contract_rows, preferred_element_type=jnp.float32
    )
    whole_grad = lax.psum(local_grad, ("gx", "gy"))
    qkv_grad = lax.dynamic_slice_in_dim(
        whole_grad, lax.axis_index("gy") * shard_rows, shard_rows, 0
    )
    return (block_out, qkv_grad)


def solution(mesh):
    in_specs = (
        P("gx", "gy", None, None),
        P("gx", "gy", None, None),
        P(),
        P("gy", None),
        P("gy", None),
    )
    out_specs = (P("gx", "gy", None, None), P("gy", None))
    return jax.shard_map(shards, mesh=mesh, in_specs=in_specs, out_specs=out_specs, check_vma=False)
```

profile of v0, /device:TPU:0, one launch (start us, length us, event | category | flops | bytes accessed | tf_op | source)
XLA Modules:
  0.0 313.7 jit_solution(8115496946814767307)
XLA Ops:
  8.0 1.3 convert_reduce_fusion
  10.7 4.6 %collective-permute-start = (bf16[4,8,8,768]{3,2,1,0:T(8,128)(2,1)S(1)}, bf16[4,8,8,768]{3,2,1,0:T(8,128)(2,1)S(1)}, u32[]{:S(2)}, u32[]{:S(2)}) collective-permute-start(bf16[4,8,8,768]{3,2,1,0:T(8,128)(2,1)S(1)} %get-tuple-element.239), channel_id=1, source_target_pairs={{0,28},{4,0},{8,4},{12,8},{16,12},{20,16},{24,20},{28,24},{1,29},{... | collective-permute-start | bytes 1179656 | tf_op jit(solution)/shard_map/ppermute | solution.py:15
  15.3 5.3 %collective-permute-done = bf16[4,8,8,768]{3,2,1,0:T(8,128)(2,1)S(1)} collective-permute-done((bf16[4,8,8,768]{3,2,1,0:T(8,128)(2,1)S(1)}, bf16[4,8,8,768]{3,2,1,0:T(8,128)(2,1)S(1)}, u32[]{:S(2)}, u32[]{:S(2)}) %collective-permute-start) | collective-permute-done | bytes 393248 | tf_op jit(solution)/shard_map/ppermute | solution.py:15
  20.7 2.5 collective-permute-start.1
  23.2 18.8 %all_gather.7 = bf16[384,768]{1,0:T(8,128)(2,1)} all-gather(bf16[96,768]{1,0:T(8,128)(2,1)S(1)} %copy-done.3), channel_id=1, replica_groups=mesh['gx'=8,'gy'=4] {'gy'}, dimensions={0}, use_global_device_ids=true | all-gather | bytes 737280 | tf_op jit(solution)/shard_map/all_gather | solution.py:98
  42.0 13.0 %all-gather.2.cloned.1.call-done = bf16[768,1152]{1,0:T(8,128)(2,1)} async-done(((bf16[192,1152]{1,0:T(8,128)(2,1)}), bf16[768,1152]{1,0:T(8,128)(2,1)}) %all-gather.2.cloned.1.call-update) | async-done | bytes 1769488 | tf_op jit(solution)/shard_map/all_gather | solution.py:78
  55.0 2.7 fusion.43
  57.7 11.2 %while.30 = (s32[]{:T(128)}, bf16[1,512,384]{1,2,0:T(8,128)(2,1)S(1)}, bf16[1,512,1152]{2,1,0:T(8,128)(2,1)S(1)}, s32[]{:T(128)}, s32[]{:T(128)}, /*index=5*/s32...) while((s32[]{:T(128)}, bf16[1,512,384]{1,2,0:T(8,128)(2,1)S(1)}, ...), condition=%wide.region_5.6_spmd, body=%wide.region_2.5_spmd.sunk | while | flops 35404812 | bytes 3582236 | solution.py:92
  68.9 1.7 convolution_convert_fusion.3
  70.7 9.0 %collective-permute-done.2 = bf16[4,8,8,768]{3,2,1,0:T(8,128)(2,1)S(1)} collective-permute-done((bf16[4,8,8,768]{3,2,1,0:T(8,128)(2,1)S(1)}, bf16[4,8,8,768]{3,2,1,0:T(8,128)(2,1)S(1)}, u32[]{:S(2)}, u32[]{:S(2)}) %collective-permute-start.2) | collective-permute-done | bytes 393248 | tf_op jit(solution)/shard_map/ppermute | solution.py:15
  79.7 1.5 collective-permute-start.3
  81.3 7.8 %collective-permute-done.3 = bf16[8,4,8,768]{3,2,1,0:T(8,128)(2,1)S(1)} collective-permute-done((bf16[8,4,8,768]{3,2,1,0:T(8,128)(2,1)S(1)}, bf16[8,4,8,768]{3,2,1,0:T(8,128)(2,1)S(1)}, u32[]{:S(2)}, u32[]{:S(2)}) %collective-permute-start.3) | collective-permute-done | bytes 393248 | tf_op jit(solution)/shard_map/ppermute | solution.py:15
  90.3 1.5 multiply_convert_fusion.1
  92.5 5.3 %collective-permute-done.4 = bf16[4,8,8,768]{3,2,1,0:T(8,128)(2,1)S(1)} collective-permute-done((bf16[4,8,8,768]{3,2,1,0:T(8,128)(2,1)S(1)}, bf16[4,8,8,768]{3,2,1,0:T(8,128)(2,1)S(1)}, u32[]{:S(2)}, u32[]{:S(2)}) %collective-permute-start.4) | collective-permute-done | bytes 393248 | tf_op jit(solution)/shard_map/ppermute | solution.py:15
  98.5 10.7 %collective-permute-done.5 = bf16[8,4,8,768]{3,2,1,0:T(8,128)(2,1)} collective-permute-done((bf16[8,4,8,768]{3,2,1,0:T(8,128)(2,1)S(1)}, bf16[8,4,8,768]{3,2,1,0:T(8,128)(2,1)}, u32[]{:S(2)}, u32[]{:S(2)}) %collective-permute-start.5) | collective-permute-done | bytes 393248 | tf_op jit(solution)/shard_map/ppermute | solution.py:15
  109.2 1.1 pad_maximum_fusion.3
  110.9 1.1 broadcast_in_dim.25
  112.0 49.0 %while.31 = (s32[]{:T(128)}, bf16[1,512,1152]{1,2,0:T(8,128)(2,1)}, bf16[1,512,1152]{2,1,0:T(8,128)(2,1)S(1)}, bf16[1,512,384]{2,1,0:T(8,128)(2,1)S(1)}, s32[]{:...) while((s32[]{:T(128)}, bf16[1,512,1152]{1,2,0:T(8,128)(2,1)}, ...), condition=%wide.region_10.11_spmd, body=%wide.region_6.10_spmd.sunk | while | flops 88160776 | bytes 9951548 | solution.py:150
  114.2 0.9 fusion.101
  118.3 0.9 fusion.101
  122.4 0.9 fusion.101
  130.5 0.9 fusion.101
  134.6 1.0 fusion.101
  138.7 0.9 fusion.101
  142.8 0.9 fusion.101
  146.9 0.9 fusion.101
  151.0 0.9 fusion.101
  155.0 0.9 fusion.101
  159.1 0.9 fusion.101
  161.0 4.2 %fusion.50 = f32[768,1152]{1,0:T(8,128)} fusion(bf16[512,768]{1,0:T(8,128)(2,1)S(1)} %bitcast.110, bf16[1,512,1152]{1,2,0:T(8,128)(2,1)} %get-tuple-element.203), kind=kOutput, calls=%fused_computation.66 | convolution fusion | flops 905969664 | bytes 5505024 | tf_op jit(solution)/shard_map/dot_general | solution.py:159
  165.3 139.4 %all-reduce.2.cloned.1.call-done = f32[768,1152]{1,0:T(8,128)} async-done(((f32[768,1152]{1,0:T(8,128)}), f32[768,1152]{1,0:T(8,128)}) %all-reduce.2.cloned.1.call-update) | async-done | bytes 3538960 | tf_op jit(solution)/shard_map/psum | solution.py:162
  304.7 2.1 constant_dynamic-slice_fusion
  (144 shorter events, 55.2 us)
Async XLA Ops:
  7.2 2.1 copy-start
  7.2 2.5 copy-start.4
  7.2 47.9 %all-gather.2.cloned.1.call-start = ((), (), s32[]{:S(2)}) async-start(), calls=%async_computation | async-start | bytes 2211840 | tf_op jit(solution)/shard_map/all_gather | solution.py:78
  7.9 296.8 %all-reduce.2.cloned.1.call-start = ((), (), s32[]{:S(2)}) async-start(), calls=%async_computation.1 | async-start | bytes 7077888 | tf_op jit(solution)/shard_map/psum | solution.py:162
  10.7 12.5 %copy-start.3 = (bf16[96,768]{1,0:T(8,128)(2,1)S(1)}, bf16[96,768]{1,0:T(8,128)(2,1)}, u32[]{:S(2)}) copy-start(bf16[96,768]{1,0:T(8,128)(2,1)} %param.13) | copy-start | bytes 442372
  10.7 9.9 %collective-permute-start = (bf16[4,8,8,768]{3,2,1,0:T(8,128)(2,1)S(1)}, bf16[4,8,8,768]{3,2,1,0:T(8,128)(2,1)S(1)}, u32[]{:S(2)}, u32[]{:S(2)}) collective-permute-start(bf16[4,8,8,768]{3,2,1,0:T(8,128)(2,1)S(1)} %get-tuple-element.239), channel_id=1, source_target_pairs={{0,28},{4,0},{8,4},{12,8},{16,12},{20,16},{24,20},{28,24},{1,29},{... | collective-permute-start | bytes 1179656 | tf_op jit(solution)/shard_map/ppermute | solution.py:15
  20.7 21.3 %collective-permute-start.1 = (bf16[8,4,8,768]{3,2,1,0:T(8,128)(2,1)S(1)}, bf16[8,4,8,768]{3,2,1,0:T(8,128)(2,1)S(1)}, u32[]{:S(2)}, u32[]{:S(2)}) collective-permute-start(bf16[8,4,8,768]{3,2,1,0:T(8,128)(2,1)S(1)} %get-tuple-element.237), channel_id=1, source_target_pairs={{0,3},{1,0},{2,1},{3,2},{4,7},{5,4},{6,5},{7,6},{8,11},{9,8},{10,9... | collective-permute-start | bytes 1179656 | tf_op jit(solution)/shard_map/ppermute | solution.py:15
  70.7 9.1 %collective-permute-start.2 = (bf16[4,8,8,768]{3,2,1,0:T(8,128)(2,1)S(1)}, bf16[4,8,8,768]{3,2,1,0:T(8,128)(2,1)S(1)}, u32[]{:S(2)}, u32[]{:S(2)}) collective-permute-start(bf16[4,8,8,768]{3,2,1,0:T(8,128)(2,1)S(1)} %bitcast.114), channel_id=1, source_target_pairs={{0,4},{4,8},{8,12},{12,16},{16,20},{20,24},{24,28},{28,0},{1,5},{5... | collective-permute-start | bytes 1179656 | tf_op jit(solution)/shard_map/ppermute | solution.py:15
  79.7 9.3 %collective-permute-start.3 = (bf16[8,4,8,768]{3,2,1,0:T(8,128)(2,1)S(1)}, bf16[8,4,8,768]{3,2,1,0:T(8,128)(2,1)S(1)}, u32[]{:S(2)}, u32[]{:S(2)}) collective-permute-start(bf16[8,4,8,768]{3,2,1,0:T(8,128)(2,1)S(1)} %fusion.55), channel_id=1, source_target_pairs={{0,1},{1,2},{2,3},{3,0},{4,5},{5,6},{6,7},{7,4},{8,9},{9,10},{10,1... | collective-permute-start | bytes 1179656 | tf_op jit(solution)/shard_map/ppermute | solution.py:15
  89.1 1.1 copy-start.2
  92.5 5.4 %collective-permute-start.4 = (bf16[4,8,8,768]{3,2,1,0:T(8,128)(2,1)S(1)}, bf16[4,8,8,768]{3,2,1,0:T(8,128)(2,1)S(1)}, u32[]{:S(2)}, u32[]{:S(2)}) collective-permute-start(bf16[4,8,8,768]{3,2,1,0:T(8,128)(2,1)S(1)} %get-tuple-element.229), channel_id=1, source_target_pairs={{0,28},{4,0},{8,4},{12,8},{16,12},{20,16},{24,20},{28,24},{1,29},{... | collective-permute-start | bytes 1179656 | tf_op jit(solution)/shard_map/ppermute | solution.py:15
  97.9 12.4 %copy-start.1 = (bf16[384,768]{1,0:T(8,128)(2,1)S(1)}, bf16[384,768]{1,0:T(8,128)(2,1)}, u32[]{:S(2)}) copy-start(bf16[384,768]{1,0:T(8,128)(2,1)} %all_gather.7) | copy-start | bytes 1769476
  97.9 11.4 %collective-permute-start.5 = (bf16[8,4,8,768]{3,2,1,0:T(8,128)(2,1)S(1)}, bf16[8,4,8,768]{3,2,1,0:T(8,128)(2,1)}, u32[]{:S(2)}, u32[]{:S(2)}) collective-permute-start(bf16[8,4,8,768]{3,2,1,0:T(8,128)(2,1)S(1)} %get-tuple-element.227), channel_id=1, source_target_pairs={{0,3},{1,0},{2,1},{3,2},{4,7},{5,4},{6,5},{7,6},{8,11},{9,8},{10,9... | collective-permute-start | bytes 1179656 | tf_op jit(solution)/shard_map/ppermute | solution.py:15
Sparse Core Ops, SparseCore 0:
  9.8 45.1 all-gather.1
  165.4 139.2 all-reduce.1
where the time goes:
time: 314 us
  waiting for transfers between devices  191 us (61%)
  matrix products  60.9 us (19%)
  blocking collectives  18.8 us (6%)
  between operations  14.3 us (5%)
  other arithmetic  13.7 us (4%)
  starting transfers between devices  9.39 us (3%)
  local copies, waits for them, and re-layouts  5.15 us (2%)
    psum x1, waiting for transfers between devices, shards(): whole_grad = lax.psum(local_grad, ('gx', 'gy'))  139 us
    ppermute x6, waiting for transfers between devices, shifted(): lax.ppermute(x, axis, [(i, (i + by) % devices) for i in range(devices)])  38.1 us
    all_gather x1, blocking collectives, shards(): proj_whole = lax.all_gather(proj_weight, 'gy', axis=0, tiled=True)  18.8 us
    all_gather x1, waiting for transfers between devices, shards(): qkv_whole = lax.all_gather(qkv_weight, 'gy', axis=0, tiled=True)  13 us
    dot_general x12, matrix products, backward_head(): jnp.einsum('wqk,wqd->wkd', grad_scores, queries, preferred_element_type=j...  11.3 us
    dot_general x12, matrix products, backward_head(): jnp.einsum('wqk,wqd->wkd', prob_half, grad_mixed, preferred_element_type=...  11.2 us
    dot_general x12, matrix products, backward_head(): jnp.einsum('wqk,wkd->wqd', grad_scores, keys_in, preferred_element_type=j...  11 us
    dot_general x24, matrix products, head_probs(): jnp.einsum('wqd,wkd->wqk', queries, keys_in, preferred_element_type=jnp.f...  9.39 us
  transfers between devices with their start and end apart: 8, of which 7 were waited for; matrix products, arithmetic and copies ran while one was open for 1% of the time, Pallas kernels for 0%

commit v1 on v0

--- a/solution.py
+++ b/solution.py
@@ -95,7 +95,31 @@
         forward_head,
         jnp.zeros((window_count, window_tokens, inner_dim), jnp.bfloat16),
     )
-    proj_whole = lax.all_gather(proj_weight, "gy", axis=0, tiled=True)
+    x_next = lax.axis_size("gy")
+    found_now = lax.axis_index("gy")
+    back, lower, y_new = (x_next, found_now, proj_weight.shape[0])
+    by_rank = []
+    for d in range(back):
+        by_rank.append((d, (d + 1) % back))
+    frames = []
+    for d in range(back):
+        frames.append((d, (d - 1) % back))
+    proj_whole = jnp.zeros(
+        (*proj_weight.shape[:0], back * y_new, *proj_weight.shape[1:]), proj_weight.dtype
+    )
+    proj_whole = lax.dynamic_update_slice_in_dim(proj_whole, proj_weight, lower * y_new, axis=0)
+    state_next = later = proj_weight
+    local_next = back // 2
+    for rr in range(1, local_next + 1):
+        state_next = lax.ppermute(state_next, "gy", by_rank)
+        proj_whole = lax.dynamic_update_slice_in_dim(
+            proj_whole, state_next, (lower - rr) % back * y_new, axis=0
+        )
+        if rr < back - local_next:
+            later = lax.ppermute(later, "gy", frames)
+            proj_whole = lax.dynamic_update_slice_in_dim(
+                proj_whole, later, (lower + rr) % back * y_new, axis=0
+            )
     contract_cols = (((1,), (1,)), ((), ()))
     block_shift = jnp.dot(
         attn_out.reshape(-1, inner_dim), proj_whole, preferred_element_type=jnp.float32

time: 314 us -> 287 us (0.914)
  matrix products: 60.9 us -> 37.1 us
  blocking collectives: 18.8 us -> 0 us
  waiting for transfers between devices: 191 us -> 203 us
  starting transfers between devices: 9.39 us -> 14.3 us
    all_gather x1 -> x0, blocking collectives: 18.8 us -> none  [shards(): proj_whole = lax.all_gather(proj_weight, 'gy', axis=0, tiled=True)]
    ppermute x0 -> x3, waiting for transfers between devices: none -> 14.3 us  [the longest x2 14.3 us: shards(): state_next = lax.ppermute(state_next, 'gy', by_rank)]
    dot_general x12, matrix products: 11 us -> 3.62 us  [backward_head(): jnp.einsum('wqk,wkd->wqd', grad_scores, keys_in, preferred_element_type=j...]
    dot_general x12, matrix products: 11.3 us -> 3.94 us  [backward_head(): jnp.einsum('wqk,wqd->wkd', grad_scores, queries, preferred_element_type=j...]
    dot_general x12, matrix products: 11.2 us -> 4.18 us  [backward_head(): jnp.einsum('wqk,wqd->wkd', prob_half, grad_mixed, preferred_element_type=...]
    ppermute x0 -> x3, starting transfers between devices: none -> 4.93 us  [the longest x2 2.48 us: shards(): state_next = lax.ppermute(state_next, 'gy', by_rank)]
  transfers between devices with their start and end apart: 8 -> 11, of which waited for: 7 -> 9; matrix products, arithmetic and copies ran while one was open for 1% -> 1% of each run, Pallas kernels for 0% -> 0%
where the time goes in v1:
time: 287 us
  waiting for transfers between devices  203 us (71%)
  matrix products  37.1 us (13%)
  starting transfers between devices  14.3 us (5%)
  between operations  14.3 us (5%)
  other arithmetic  13.7 us (5%)
  local copies, waits for them, and re-layouts  4.22 us (1%)
    psum x1, waiting for transfers between devices, shards(): whole_grad = lax.psum(local_grad, ('gx', 'gy'))  139 us
    ppermute x6, waiting for transfers between devices, shifted(): lax.ppermute(x, axis, [(i, (i + by) % devices) for i in range(devices)])  35.6 us
    ppermute x2, waiting for transfers between devices, shards(): state_next = lax.ppermute(state_next, 'gy', by_rank)  14.3 us
    all_gather x1, waiting for transfers between devices, shards(): qkv_whole = lax.all_gather(qkv_weight, 'gy', axis=0, tiled=True)  12.7 us
    dot_general x24, matrix products, head_probs(): jnp.einsum('wqd,wkd->wqk', queries, keys_in, preferred_element_type=jnp.f...  9.61 us
    ppermute x6, starting transfers between devices, shifted(): lax.ppermute(x, axis, [(i, (i + by) % devices) for i in range(devices)])  9.31 us
  transfers between devices with their start and end apart: 11, of which 9 were waited for; matrix products, arithmetic and copies ran while one was open for 1% of the time, Pallas kernels for 0%

profile of v1, /device:TPU:0, one launch (start us, length us, event | category | flops | bytes accessed | tf_op | source)
XLA Modules:
  0.0 286.5 jit_solution(16184020242296857866)
XLA Ops:
  7.2 0.7 all-gather.2.cloned.1.call-update
  8.0 1.3 convert_reduce_fusion
  10.7 4.6 %collective-permute-start = (bf16[4,8,8,768]{3,2,1,0:T(8,128)(2,1)S(1)}, bf16[4,8,8,768]{3,2,1,0:T(8,128)(2,1)S(1)}, u32[]{:S(2)}, u32[]{:S(2)}) collective-permute-start(bf16[4,8,8,768]{3,2,1,0:T(8,128)(2,1)S(1)} %get-tuple-element.239), channel_id=1, source_target_pairs={{0,28},{4,0},{8,4},{12,8},{16,12},{20,16},{24,20},{28,24},{1,29},{... | collective-permute-start | bytes 1179656 | tf_op jit(solution)/shard_map/ppermute | solution.py:15
  15.3 2.4 collective-permute-start.3
  17.8 2.8 collective-permute-done
  20.7 2.5 collective-permute-start.1
  23.3 2.4 collective-permute-done.2
  25.7 2.5 collective-permute-start.4
  28.2 11.9 %collective-permute-done.4 = bf16[96,768]{1,0:T(8,128)(2,1)S(1)} collective-permute-done((bf16[96,768]{1,0:T(8,128)(2,1)S(1)}, bf16[96,768]{1,0:T(8,128)(2,1)S(1)}, u32[]{:S(2)}, u32[]{:S(2)}) %collective-permute-start.4) | collective-permute-done | bytes 147488 | tf_op jit(solution)/shard_map/ppermute | solution.py:114
  40.2 12.7 %all-gather.2.cloned.1.call-done = bf16[768,1152]{1,0:T(8,128)(2,1)} async-done(((bf16[192,1152]{1,0:T(8,128)(2,1)}), bf16[768,1152]{1,0:T(8,128)(2,1)}) %all-gather.2.cloned.1.call-update) | async-done | bytes 1769488 | tf_op jit(solution)/shard_map/all_gather | solution.py:78
  52.9 2.7 fusion.43
  55.6 11.1 %while.30 = (s32[]{:T(128)}, bf16[1,512,384]{1,2,0:T(8,128)(2,1)S(1)}, bf16[1,512,1152]{2,1,0:T(8,128)(2,1)S(1)}, s32[]{:T(128)}, s32[]{:T(128)}, /*index=5*/s32...) while((s32[]{:T(128)}, bf16[1,512,384]{1,2,0:T(8,128)(2,1)S(1)}, ...), condition=%wide.region_5.6_spmd, body=%wide.region_2.5_spmd.sunk | while | flops 35404812 | bytes 3582228 | solution.py:92
  66.7 0.6 convolution_convert_fusion.3
  67.4 9.0 %collective-permute-done.5 = bf16[4,8,8,768]{3,2,1,0:T(8,128)(2,1)S(1)} collective-permute-done((bf16[4,8,8,768]{3,2,1,0:T(8,128)(2,1)S(1)}, bf16[4,8,8,768]{3,2,1,0:T(8,128)(2,1)S(1)}, u32[]{:S(2)}, u32[]{:S(2)}) %collective-permute-start.5) | collective-permute-done | bytes 393248 | tf_op jit(solution)/shard_map/ppermute | solution.py:15
  76.5 1.5 collective-permute-start.6
  78.0 7.8 %collective-permute-done.6 = bf16[8,4,8,768]{3,2,1,0:T(8,128)(2,1)S(1)} collective-permute-done((bf16[8,4,8,768]{3,2,1,0:T(8,128)(2,1)S(1)}, bf16[8,4,8,768]{3,2,1,0:T(8,128)(2,1)S(1)}, u32[]{:S(2)}, u32[]{:S(2)}) %collective-permute-start.6) | collective-permute-done | bytes 393248 | tf_op jit(solution)/shard_map/ppermute | solution.py:15
  86.2 0.8 copy-done.1
  87.0 1.5 multiply_convert_fusion.1
  89.2 5.3 %collective-permute-done.7 = bf16[4,8,8,768]{3,2,1,0:T(8,128)(2,1)S(1)} collective-permute-done((bf16[4,8,8,768]{3,2,1,0:T(8,128)(2,1)S(1)}, bf16[4,8,8,768]{3,2,1,0:T(8,128)(2,1)S(1)}, u32[]{:S(2)}, u32[]{:S(2)}) %collective-permute-start.7) | collective-permute-done | bytes 393248 | tf_op jit(solution)/shard_map/ppermute | solution.py:15
  94.6 0.6 collective-permute-start.8
  95.2 10.7 %collective-permute-done.8 = bf16[8,4,8,768]{3,2,1,0:T(8,128)(2,1)} collective-permute-done((bf16[8,4,8,768]{3,2,1,0:T(8,128)(2,1)S(1)}, bf16[8,4,8,768]{3,2,1,0:T(8,128)(2,1)}, u32[]{:S(2)}, u32[]{:S(2)}) %collective-permute-start.8) | collective-permute-done | bytes 393248 | tf_op jit(solution)/shard_map/ppermute | solution.py:15
  105.9 1.1 pad_maximum_fusion.3
  107.0 0.6 fusion.49
  107.7 27.5 %while.31 = (s32[]{:T(128)}, bf16[1,512,1152]{1,2,0:T(8,128)(2,1)S(1)}, bf16[1,512,1152]{2,1,0:T(8,128)(2,1)S(1)}, bf16[1,512,384]{2,1,0:T(8,128)(2,1)S(1)}, s32...) while((s32[]{:T(128)}, ...), condition=%wide.region_10.11_spmd, body=%wide.region_6.10_spmd.sunk | while | flops 88160776 | bytes 9951540 | solution.py:174
  108.3 0.4 multiply_reduce_fusion.2
  110.6 0.4 multiply_reduce_fusion.2
  112.9 0.4 multiply_reduce_fusion.2
  115.2 0.4 multiply_reduce_fusion.2
  117.5 0.4 multiply_reduce_fusion.2
  135.2 3.0 %fusion.50 = f32[768,1152]{1,0:T(8,128)} fusion(bf16[512,768]{1,0:T(8,128)(2,1)S(1)} %bitcast.110, bf16[1,512,1152]{1,2,0:T(8,128)(2,1)S(1)} %get-tuple-element.203), kind=kOutput, calls=%fused_computation.66 | convolution fusion | flops 905969664 | bytes 5505024 | tf_op jit(solution)/shard_map/dot_general | solution.py:183
  138.2 139.3 %all-reduce.2.cloned.1.call-done = f32[768,1152]{1,0:T(8,128)} async-done(((f32[768,1152]{1,0:T(8,128)}), f32[768,1152]{1,0:T(8,128)}) %all-reduce.2.cloned.1.call-update) | async-done | bytes 3538960 | tf_op jit(solution)/shard_map/psum | solution.py:186
  277.5 2.1 constant_dynamic-slice_fusion
  (152 shorter events, 39.6 us)
Async XLA Ops:
  7.2 2.1 copy-start
  7.2 2.5 copy-start.3
  7.2 45.7 %all-gather.2.cloned.1.call-start = ((), (), s32[]{:S(2)}) async-start(), calls=%async_computation | async-start | bytes 2211840 | tf_op jit(solution)/shard_map/all_gather | solution.py:78
  7.9 269.6 %all-reduce.2.cloned.1.call-start = ((), (), s32[]{:S(2)}) async-start(), calls=%async_computation.1 | async-start | bytes 7077888 | tf_op jit(solution)/shard_map/psum | solution.py:186
  10.3 5.0 %copy-start.2 = (bf16[96,768]{1,0:T(8,128)(2,1)S(1)}, bf16[96,768]{1,0:T(8,128)(2,1)}, u32[]{:S(2)}) copy-start(bf16[96,768]{1,0:T(8,128)(2,1)} %param.13) | copy-start | bytes 442372
  10.7 9.9 %collective-permute-start = (bf16[4,8,8,768]{3,2,1,0:T(8,128)(2,1)S(1)}, bf16[4,8,8,768]{3,2,1,0:T(8,128)(2,1)S(1)}, u32[]{:S(2)}, u32[]{:S(2)}) collective-permute-start(bf16[4,8,8,768]{3,2,1,0:T(8,128)(2,1)S(1)} %get-tuple-element.239), channel_id=1, source_target_pairs={{0,28},{4,0},{8,4},{12,8},{16,12},{20,16},{24,20},{28,24},{1,29},{... | collective-permute-start | bytes 1179656 | tf_op jit(solution)/shard_map/ppermute | solution.py:15
  15.3 12.9 %collective-permute-start.3 = (bf16[96,768]{1,0:T(8,128)(2,1)S(1)}, bf16[96,768]{1,0:T(8,128)(2,1)S(1)}, u32[]{:S(2)}, u32[]{:S(2)}) collective-permute-start(bf16[96,768]{1,0:T(8,128)(2,1)S(1)} %copy-done.2), channel_id=1, source_target_pairs={{0,3},{1,0},{2,1},{3,2},{4,7},{5,4},{6,5},{7,6},{8,11},{9,8},{10,9... | collective-permute-start | bytes 442376 | tf_op jit(solution)/shard_map/ppermute | solution.py:119
  17.8 7.9 %collective-permute-start.2 = (bf16[96,768]{1,0:T(8,128)(2,1)S(1)}, bf16[96,768]{1,0:T(8,128)(2,1)S(1)}, u32[]{:S(2)}, u32[]{:S(2)}) collective-permute-start(bf16[96,768]{1,0:T(8,128)(2,1)S(1)} %copy-done.2), channel_id=1, source_target_pairs={{0,1},{1,2},{2,3},{3,0},{4,5},{5,6},{6,7},{7,4},{8,9},{9,10},{10,1... | collective-permute-start | bytes 442376 | tf_op jit(solution)/shard_map/ppermute | solution.py:114
  20.7 19.5 %collective-permute-start.1 = (bf16[8,4,8,768]{3,2,1,0:T(8,128)(2,1)S(1)}, bf16[8,4,8,768]{3,2,1,0:T(8,128)(2,1)S(1)}, u32[]{:S(2)}, u32[]{:S(2)}) collective-permute-start(bf16[8,4,8,768]{3,2,1,0:T(8,128)(2,1)S(1)} %get-tuple-element.237), channel_id=1, source_target_pairs={{0,3},{1,0},{2,1},{3,2},{4,7},{5,4},{6,5},{7,6},{8,11},{9,8},{10,9... | collective-permute-start | bytes 1179656 | tf_op jit(solution)/shard_map/ppermute | solution.py:15
  25.7 14.4 %collective-permute-start.4 = (bf16[96,768]{1,0:T(8,128)(2,1)S(1)}, bf16[96,768]{1,0:T(8,128)(2,1)S(1)}, u32[]{:S(2)}, u32[]{:S(2)}) collective-permute-start(bf16[96,768]{1,0:T(8,128)(2,1)S(1)} %collective-permute-done.2), channel_id=1, source_target_pairs={{0,1},{1,2},{2,3},{3,0},{4,5},{5,6},{6,7},{7,4},{8,9},{9,10},{10,1... | collective-permute-start | bytes 442376 | tf_op jit(solution)/shard_map/ppermute | solution.py:114
  67.4 9.1 %collective-permute-start.5 = (bf16[4,8,8,768]{3,2,1,0:T(8,128)(2,1)S(1)}, bf16[4,8,8,768]{3,2,1,0:T(8,128)(2,1)S(1)}, u32[]{:S(2)}, u32[]{:S(2)}) collective-permute-start(bf16[4,8,8,768]{3,2,1,0:T(8,128)(2,1)S(1)} %bitcast.114), channel_id=1, source_target_pairs={{0,4},{4,8},{8,12},{12,16},{16,20},{20,24},{24,28},{28,0},{1,5},{5... | collective-permute-start | bytes 1179656 | tf_op jit(solution)/shard_map/ppermute | solution.py:15
  76.5 9.3 %collective-permute-start.6 = (bf16[8,4,8,768]{3,2,1,0:T(8,128)(2,1)S(1)}, bf16[8,4,8,768]{3,2,1,0:T(8,128)(2,1)S(1)}, u32[]{:S(2)}, u32[]{:S(2)}) collective-permute-start(bf16[8,4,8,768]{3,2,1,0:T(8,128)(2,1)S(1)} %fusion.55), channel_id=1, source_target_pairs={{0,1},{1,2},{2,3},{3,0},{4,5},{5,6},{6,7},{7,4},{8,9},{9,10},{10,1... | collective-permute-start | bytes 1179656 | tf_op jit(solution)/shard_map/ppermute | solution.py:15
  85.8 1.1 copy-start.1
  89.2 5.4 %collective-permute-start.7 = (bf16[4,8,8,768]{3,2,1,0:T(8,128)(2,1)S(1)}, bf16[4,8,8,768]{3,2,1,0:T(8,128)(2,1)S(1)}, u32[]{:S(2)}, u32[]{:S(2)}) collective-permute-start(bf16[4,8,8,768]{3,2,1,0:T(8,128)(2,1)S(1)} %get-tuple-element.229), channel_id=1, source_target_pairs={{0,28},{4,0},{8,4},{12,8},{16,12},{20,16},{24,20},{28,24},{1,29},{... | collective-permute-start | bytes 1179656 | tf_op jit(solution)/shard_map/ppermute | solution.py:15
  94.6 11.3 %collective-permute-start.8 = (bf16[8,4,8,768]{3,2,1,0:T(8,128)(2,1)S(1)}, bf16[8,4,8,768]{3,2,1,0:T(8,128)(2,1)}, u32[]{:S(2)}, u32[]{:S(2)}) collective-permute-start(bf16[8,4,8,768]{3,2,1,0:T(8,128)(2,1)S(1)} %get-tuple-element.227), channel_id=1, source_target_pairs={{0,3},{1,0},{2,1},{3,2},{4,7},{5,4},{6,5},{7,6},{8,11},{9,8},{10,9... | collective-permute-start | bytes 1179656 | tf_op jit(solution)/shard_map/ppermute | solution.py:15
Sparse Core Ops, SparseCore 0:
  9.8 43.0 all-gather.1
  138.4 139.1 all-reduce.1
